TPU v7x, 32 devices: a whole 2x2x4 slice. The times are simulated.
32 devices in a mesh: cells: 8 (over y, x, core), modes: 4 (over z).
Axes of the slice: x: 2, y: 2, z: 4, core: 2. Of those that a mesh axis runs over, the one named last changes fastest.
Arguments:
- phonons: float32 [8, 8, 8, 16, 6144], P('cells', None, None, None, 'modes'), may hold values from -6 to 6
- heaters: int32 [8, 8, 8, 16], P('cells'), may hold values 0 or 1
- courant: float32 [3, 6144], P(None, 'modes'), may hold values from 0.05 to 0.3
- upwind: int32 [3, 6144], P(None, 'modes'), may hold values from 0 to 1
- relaxation: float32 [6144], P('modes'), may hold values from 0.02 to 0.4
- source: float32 [6144], P('modes'), may hold values from -6 to 6
- coupling: bfloat16 [6144, 6144], P('modes'), may hold values from -0.0390625 to 0.0390625
Outputs:
- evolved: float32 [8, 8, 8, 16, 6144], P('cells', None, None, None, 'modes')
All inputs are finite; a program needn't handle non-finite values. No bound on the sum of `heaters` on one device may be relied on, other than what follows from the above.
Results may differ from a plain program's by a relative error of at most 0.0018.
Values may be sent and summed in bfloat16 or wider, within the bound.
A program may use at most 128 MiB of HBM per device.

v0:
```python
import jax
import jax.numpy as jnp
from jax import lax
from jax.sharding import PartitionSpec as P

GY = 4
STEPS = 2


def shifted(block, axis, distance):
    devices = range(lax.axis_size(axis))
    route = [((i - distance) % len(devices), i) for i in devices]
    return lax.ppermute(block, axis, route)


def upstream(density, forward, axis):
    widths = [(0, 0)] * density.ndim
    widths[axis] = (1, 1)
    padded = jnp.pad(density, widths)
    length_axis = density.shape[axis]
    behind = lax.slice_in_dim(padded, 0, length_axis, axis=axis)
    ahead = lax.slice_in_dim(padded, 2, length_axis + 2, axis=axis)
    return jnp.where(forward, behind, ahead)


def scatter_term(rounded, coupling):
    contract = (((1,), (1,)), ((), ()))
    gathered = lax.all_gather(rounded, "modes", axis=1, tiled=True)
    return lax.dot_general(gathered, coupling, contract, preferred_element_type=jnp.float32)


def advect(density, courant, upwind, masks):
    lower_y_ok, upper_y_ok = masks
    forward_x = upwind[0] == 1
    forward_y = upwind[1] == 1
    forward_z = upwind[2] == 1
    below_x = shifted(density[-1].astype(jnp.bfloat16), "cells", GY).astype(jnp.float32)
    above_x = shifted(density[0], "cells", -GY)
    below_y = (
        shifted(density[:, -1].astype(jnp.bfloat16), "cells", 1).astype(jnp.float32) * lower_y_ok
    )
    above_y = (
        shifted(density[:, 0].astype(jnp.bfloat16), "cells", -1).astype(jnp.float32) * upper_y_ok
    )
    upstream_z = upstream(density, forward_z, 2)
    transport = courant[0] * (density - upstream(density, forward_x, 0))
    transport = transport + courant[1] * (density - upstream(density, forward_y, 1))
    transport = transport + courant[2] * (density - upstream_z)
    transport = transport.at[0].add(-courant[0] * jnp.where(forward_x, below_x, 0.0))
    transport = transport.at[-1].add(-courant[0] * jnp.where(forward_x, 0.0, above_x))
    transport = transport.at[:, 0].add(-courant[1] * jnp.where(forward_y, below_y, 0.0))
    transport = transport.at[:, -1].add(-courant[1] * jnp.where(forward_y, 0.0, above_y))
    return transport


def per_device(phonons, heaters, courant, upwind, relaxation, source, coupling):
    density = phonons[0]
    cell_count = density.shape[0] * density.shape[1] * density.shape[2]
    mode_count = density.shape[3]
    block_total = lax.axis_size("cells")
    position = (lax.axis_index("cells") + 2) % block_total
    column = position % GY
    masks = ((column != 0).astype(jnp.float32), (column != GY - 1).astype(jnp.float32))
    heating = heaters[0].astype(jnp.float32)[..., None] * source
    for repeat in range(STEPS):
        rounded = density.astype(jnp.bfloat16).reshape(cell_count, mode_count)
        scattered = scatter_term(rounded, coupling).reshape(density.shape)
        transport = advect(density, courant, upwind, masks)
        density = density - transport - relaxation * density - scattered + heating
    return density[None]


def solution(mesh):
    placed = (
        P("cells", None, None, None, "modes"),
        P("cells", None, None, None),
        P(None, "modes"),
        P(None, "modes"),
        P("modes"),
        P("modes"),
        P("modes", None),
    )
    return jax.shard_map(
        per_device,
        mesh=mesh,
        in_specs=placed,
        out_specs=P("cells", None, None, None, "modes"),
        check_vma=False,
    )
```

profile of v0, /device:TPU:0, one launch (start us, length us, event | category | flops | bytes accessed | tf_op | source)
XLA Modules:
  0.0 519.6 jit_solution(12201974563363240435)
XLA Ops:
  6.5 5.0 convert.12
  12.7 3.0 collective-permute-start
  17.2 3.4 copy.37
  20.7 2.6 collective-permute-start.3
  23.5 7.2 %fusion.4 = f32[8,8,16,1536]{3,2,1,0:T(8,128)} fusion(f32[8,8,16,1536]{3,2,1,0:T(8,128)S(1)} %bitcast.82, f32[1536]{0:T(1024)S(1)} %get-tuple-element.105, f32[1536]{0:T(1024)S(1)} %get-tuple-element.106, f32[1536]{0:T(1024)S(1)} %get-tuple-element.104, pred[1536]{0:T(1024)(128)(4,1)S(1)} %get-tuple-element.102, pred[1536]{0:T(1024)(128)(4,1)S(1)} %get-tuple-element.103, ...), kind=kLoop, calls=%fused_computation.18 | loop fusion | flops 17301504 | bytes 12605952 | tf_op jit(solution)/shard_map/add | solution.py:48
  31.5 1.4 convert_bitcast_fusion
  32.9 2.3 fusion.35
  35.2 6.2 %copy.16 = f32[8,8,16,1536]{3,2,0,1:T(8,128)} copy(f32[8,8,16,1536]{3,2,1,0:T(8,128)} %fusion.35) | data formatting | bytes 12582912 | tf_op jit(solution)/shard_map/scatter-add | solution.py:49
  41.4 4.5 collective-permute-done.1
  45.9 2.2 fusion.34
  48.1 2.2 fusion.32
  50.3 2.1 fusion.31
  52.4 180.2 %all-gather.3.cloned.1.call-done = bf16[1024,6144]{1,0:T(8,128)(2,1)} async-done(((bf16[1024,1536]{1,0:T(8,128)(2,1)}), bf16[1024,6144]{1,0:T(8,128)(2,1)}) %all-gather.3.cloned.1.call-update) | async-done | bytes 12582928 | tf_op jit(solution)/shard_map/all_gather | solution.py:28
  232.6 24.1 %fusion.37 = f32[1024,1536]{1,0:T(8,128)S(1)} fusion(bf16[1024,6144]{1,0:T(8,128)(2,1)} %all-gather.3.cloned.1.call-done, bf16[1536,6144]{1,0:T(8,128)(2,1)} %param.29), kind=kOutput, calls=%fused_computation.77 | convolution fusion | flops 19327352832 | bytes 37748736 | tf_op jit(solution)/shard_map/dot_general | solution.py:29
  256.8 8.1 %fusion.36 = (bf16[8,8,16,1536]{3,2,1,0:T(8,128)(2,1)}, f32[8,8,16,1536]{3,2,1,0:T(8,128)}) fusion(f32[1536]{0:T(1024)S(1)} %copy-done.13, f32[8,8,16]{2,1,0:T(8,128)S(1)} %copy-done, f32[8,8,16,1536]{3,2,0,1:T(8,128)} %fusion.31, f32[8,8,16,1536]{3,2,1,0:T(8,128)S(1)} %bitcast.86, f32[1,8,8,16,1536]{4,3,2,1,0:T(8,128)} %param.23, f32[1536]{0:T(1024)S(1)} %copy-done.14), kind=kLoop, calls=%fused_computation.76 | loop fusion | flops 11010048 | bytes 28327936 | tf_op jit(solution)/shard_map/convert.2
  266.0 1.5 collective-permute-start.4
  269.4 18.0 %fusion.12 = f32[8,8,16,1536]{3,2,1,0:T(8,128)S(1)} fusion(f32[8,8,16,1536]{3,2,1,0:T(8,128)} %get-tuple-element.108, f32[1536]{0:T(1024)S(1)} %copy-done.12, f32[1536]{0:T(1024)S(1)} %copy-done.4, f32[1536]{0:T(1024)S(1)} %copy-done.2, pred[1536]{0:T(1024)(128)(4,1)S(1)} %copy-done.16, pred[1536]{0:T(1024)(128)(4,1)S(1)} %copy-done.7, ...), kind=kLoop, calls=%fused_computation.26 | loop fusion | flops 17301504 | bytes 12605952 | tf_op jit(solution)/shard_map/add | solution.py:48
  288.8 2.6 collective-permute-start.7
  292.5 4.6 collective-permute-done.5
  297.2 2.1 collective-permute-done.6
  299.5 3.0 copy.22
  303.6 177.9 %all-gather.5.cloned.1.call-done = bf16[1024,6144]{1,0:T(8,128)(2,1)} async-done(((bf16[1024,1536]{1,0:T(8,128)(2,1)}), bf16[1024,6144]{1,0:T(8,128)(2,1)}) %all-gather.5.cloned.1.call-update) | async-done | bytes 12582928 | tf_op jit(solution)/shard_map/all_gather | solution.py:28
  481.5 24.1 %fusion.38 = f32[1024,1536]{1,0:T(8,128)S(1)} fusion(bf16[1024,6144]{1,0:T(8,128)(2,1)} %all-gather.5.cloned.1.call-done, bf16[1536,6144]{1,0:T(8,128)(2,1)} %param.29), kind=kOutput, calls=%fused_computation.78 | convolution fusion | flops 19327352832 | bytes 37748736 | tf_op jit(solution)/shard_map/dot_general | solution.py:29
  505.6 7.1 %fusion.16 = f32[1,8,8,16,1536]{4,3,2,1,0:T(8,128)} fusion(f32[8,8,16,1536]{3,2,1,0:T(8,128)S(1)} %bitcast.85, f32[8,8,16,1536]{3,2,1,0:T(8,128)} %get-tuple-element.108, f32[8,8,16,1536]{3,2,1,0:T(8,128)} %fusion.26, f32[1536]{0:T(1024)S(1)} %copy-done.14, f32[1536]{0:T(1024)S(1)} %copy-done.13, f32[8,8,16]{2,1,0:T(8,128)S(1)} %copy-done), kind=kLoop, calls=%fused_computation.30 | loop fusion | flops 9437184 | bytes 25182208 | tf_op jit(solution)/shard_map/broadcast_in_dim | solution.py:70
  (71 shorter events, 10.3 us)
Async XLA Ops:
  6.5 226.1 %all-gather.3.cloned.1.call-start = ((), (), s32[]{:S(2)}) async-start(), calls=%async_computation | async-start | bytes 15728640 | tf_op jit(solution)/shard_map/all_gather | solution.py:28
  11.6 469.9 %all-gather.5.cloned.1.call-start = ((), (), s32[]{:S(2)}) async-start(), calls=%async_computation.1 | async-start | bytes 15728640 | tf_op jit(solution)/shard_map/all_gather | solution.py:28
  12.6 10.7 %copy-start.18 = (f32[3,1536]{1,0:T(4,128)S(1)}, f32[3,1536]{1,0:T(4,128)}, u32[]{:S(2)}) copy-start(f32[3,1536]{1,0:T(4,128)} %param.25) | copy-start | bytes 55300
  12.6 10.7 %copy-start.17 = (s32[3,1536]{1,0:T(4,128)S(1)}, s32[3,1536]{1,0:T(4,128)}, u32[]{:S(2)}) copy-start(s32[3,1536]{1,0:T(4,128)} %param.26) | copy-start | bytes 55300
  12.7 10.9 %slice-start = ((s8[6291456]{0:T(1024)(128)(4,1)}), s8[4194304]{0:T(1024)(128)(4,1)S(1)}, s32[]{:S(2)}) async-start(s8[6291456]{0:T(1024)(128)(4,1)} %bitcast.80), calls=%async_computation.2 | async-start | bytes 8388608
  12.7 20.2 %collective-permute-start = (bf16[8,16,1536]{2,1,0:T(8,128)(2,1)S(1)}, bf16[8,16,1536]{2,1,0:T(8,128)(2,1)}, u32[]{:S(2)}, u32[]{:S(2)}) collective-permute-start(bf16[8,16,1536]{2,1,0:T(8,128)(2,1)S(1)} %slice_bitcast_fusion.10), channel_id=1, source_target_pairs={{16,0},{20,4},{24,8},{28,12},{0,16},{4,20},{8,24},{12,28},{17,1},{... | collective-permute-start | bytes 1179656 | tf_op jit(solution)/shard_map/ppermute | solution.py:13
  16.9 29.0 %collective-permute-start.1 = (f32[8,16,1536]{2,1,0:T(8,128)S(1)}, f32[8,16,1536]{2,1,0:T(8,128)S(1)}, u32[]{:S(2)}, u32[]{:S(2)}) collective-permute-start(f32[8,16,1536]{2,1,0:T(8,128)S(1)} %slice_bitcast_fusion.4), channel_id=1, source_target_pairs={{16,0},{20,4},{24,8},{28,12},{0,16},{4,20},{8,24},{12,28},{17,1},{... | collective-permute-start | bytes 2359304 | tf_op jit(solution)/shard_map/ppermute | solution.py:13
  20.6 27.4 %collective-permute-start.2 = (bf16[8,16,1536]{2,1,0:T(8,128)(2,1)S(1)}, bf16[8,16,1536]{2,1,0:T(8,128)(2,1)S(1)}, u32[]{:S(2)}, u32[]{:S(2)}) collective-permute-start(bf16[8,16,1536]{2,1,0:T(8,128)(2,1)S(1)} %get-tuple-element.112), channel_id=1, source_target_pairs={{28,0},{0,4},{4,8},{8,12},{12,16},{16,20},{20,24},{24,28},{29,1},{... | collective-permute-start | bytes 1179656 | tf_op jit(solution)/shard_map/ppermute | solution.py:13
  20.7 29.6 %collective-permute-start.3 = (bf16[8,16,1536]{2,1,0:T(8,128)(2,1)S(1)}, bf16[8,16,1536]{2,1,0:T(8,128)(2,1)S(1)}, u32[]{:S(2)}, u32[]{:S(2)}) collective-permute-start(bf16[8,16,1536]{2,1,0:T(8,128)(2,1)S(1)} %get-tuple-element.111), channel_id=1, source_target_pairs={{4,0},{8,4},{12,8},{16,12},{20,16},{24,20},{28,24},{0,28},{5,1},{9... | collective-permute-start | bytes 1179656 | tf_op jit(solution)/shard_map/ppermute | solution.py:13
  35.2 10.7 %copy-start.9 = (pred[1536]{0:T(1024)(128)(4,1)S(1)}, pred[1536]{0:T(1024)(128)(4,1)}, u32[]{:S(2)}) copy-start(pred[1536]{0:T(1024)(128)(4,1)} %copy-done.8) | copy-start | bytes 4612
  35.2 12.9 %copy-start.6 = (pred[1536]{0:T(1024)(128)(4,1)S(1)}, pred[1536]{0:T(1024)(128)(4,1)}, u32[]{:S(2)}) copy-start(pred[1536]{0:T(1024)(128)(4,1)} %copy-done.5) | copy-start | bytes 4612
  52.4 204.3 %copy-start = (f32[8,8,16]{2,1,0:T(8,128)S(1)}, f32[8,8,16]{2,1,0:T(8,128)}, u32[]{:S(2)}) copy-start(f32[8,8,16]{2,1,0:T(8,128)} %convert_bitcast_fusion) | copy-start | bytes 12292
  52.4 204.3 %copy-start.13 = (f32[1536]{0:T(1024)S(1)}, f32[1536]{0:T(1024)}, u32[]{:S(2)}) copy-start(f32[1536]{0:T(1024)} %param.28) | copy-start | bytes 18436
  52.4 204.3 %copy-start.14 = (f32[1536]{0:T(1024)S(1)}, f32[1536]{0:T(1024)}, u32[]{:S(2)}) copy-start(f32[1536]{0:T(1024)} %param.27) | copy-start | bytes 18436
  256.8 12.6 %copy-start.2 = (f32[1536]{0:T(1024)S(1)}, f32[1536]{0:T(1024)}, u32[]{:S(2)}) copy-start(f32[1536]{0:T(1024)} %copy-done.1) | copy-start | bytes 18436
  256.8 12.6 %copy-start.4 = (f32[1536]{0:T(1024)S(1)}, f32[1536]{0:T(1024)}, u32[]{:S(2)}) copy-start(f32[1536]{0:T(1024)} %copy-done.3) | copy-start | bytes 18436
  256.8 12.6 %copy-start.7 = (pred[1536]{0:T(1024)(128)(4,1)S(1)}, pred[1536]{0:T(1024)(128)(4,1)}, u32[]{:S(2)}) copy-start(pred[1536]{0:T(1024)(128)(4,1)} %copy-done.5) | copy-start | bytes 4612
  256.8 12.6 %copy-start.10 = (pred[1536]{0:T(1024)(128)(4,1)S(1)}, pred[1536]{0:T(1024)(128)(4,1)}, u32[]{:S(2)}) copy-start(pred[1536]{0:T(1024)(128)(4,1)} %copy-done.8) | copy-start | bytes 4612
  256.8 12.6 %copy-start.12 = (f32[1536]{0:T(1024)S(1)}, f32[1536]{0:T(1024)}, u32[]{:S(2)}) copy-start(f32[1536]{0:T(1024)} %copy-done.11) | copy-start | bytes 18436
  256.8 12.6 %copy-start.16 = (pred[1536]{0:T(1024)(128)(4,1)S(1)}, pred[1536]{0:T(1024)(128)(4,1)}, u32[]{:S(2)}) copy-start(pred[1536]{0:T(1024)(128)(4,1)} %copy-done.15) | copy-start | bytes 4612
  266.0 25.5 %collective-permute-start.4 = (bf16[8,16,1536]{2,1,0:T(8,128)(2,1)S(1)}, bf16[8,16,1536]{2,1,0:T(8,128)(2,1)S(1)}, u32[]{:S(2)}, u32[]{:S(2)}) collective-permute-start(bf16[8,16,1536]{2,1,0:T(8,128)(2,1)S(1)} %slice_bitcast_fusion.7), channel_id=1, source_target_pairs={{16,0},{20,4},{24,8},{28,12},{0,16},{4,20},{8,24},{12,28},{17,1},{... | collective-permute-start | bytes 1179656 | tf_op jit(solution)/shard_map/ppermute | solution.py:13
  268.7 28.4 %collective-permute-start.5 = (f32[8,16,1536]{2,1,0:T(8,128)S(1)}, f32[8,16,1536]{2,1,0:T(8,128)S(1)}, u32[]{:S(2)}, u32[]{:S(2)}) collective-permute-start(f32[8,16,1536]{2,1,0:T(8,128)S(1)} %slice_bitcast_fusion.1), channel_id=1, source_target_pairs={{16,0},{20,4},{24,8},{28,12},{0,16},{4,20},{8,24},{12,28},{17,1},{... | collective-permute-start | bytes 2359304 | tf_op jit(solution)/shard_map/ppermute | solution.py:13
  288.6 10.7 %collective-permute-start.6 = (bf16[8,16,1536]{2,1,0:T(8,128)(2,1)S(1)}, bf16[8,16,1536]{2,1,0:T(8,128)(2,1)S(1)}, u32[]{:S(2)}, u32[]{:S(2)}) collective-permute-start(bf16[8,16,1536]{2,1,0:T(8,128)(2,1)S(1)} %get-tuple-element.110), channel_id=1, source_target_pairs={{28,0},{0,4},{4,8},{8,12},{12,16},{16,20},{20,24},{24,28},{29,1},{... | collective-permute-start | bytes 1179656 | tf_op jit(solution)/shard_map/ppermute | solution.py:13
  288.8 13.7 %collective-permute-start.7 = (bf16[8,16,1536]{2,1,0:T(8,128)(2,1)S(1)}, bf16[8,16,1536]{2,1,0:T(8,128)(2,1)S(1)}, u32[]{:S(2)}, u32[]{:S(2)}) collective-permute-start(bf16[8,16,1536]{2,1,0:T(8,128)(2,1)S(1)} %get-tuple-element.109), channel_id=1, source_target_pairs={{4,0},{8,4},{12,8},{16,12},{20,16},{24,20},{28,24},{0,28},{5,1},{9... | collective-permute-start | bytes 1179656 | tf_op jit(solution)/shard_map/ppermute | solution.py:13
  (7 other events, 50.5 us)
Sparse Core Ops, SparseCore 0:
  11.7 220.8 all-gather.2
  265.1 216.3 all-gather.4
where the time goes:
time: 520 us
  waiting for transfers between devices  369 us (71%)
  other arithmetic  58.1 us (11%)
  matrix products  48.2 us (9%)
  local copies, waits for them, and re-layouts  19.2 us (4%)
  between operations  13.8 us (3%)
  starting transfers between devices  11 us (2%)
    all_gather x2, waiting for transfers between devices, scatter_term(): gathered = lax.all_gather(rounded, 'modes', axis=1, tiled=True)  358 us
    dot_general x2, matrix products, scatter_term(): lax.dot_general(gathered, coupling, contract, preferred_element_type=jnp....  48.2 us
    add x2, other arithmetic, advect(): transport = transport + courant[2] * (density - upstream_z)  25.2 us
    another operation x2, other arithmetic  13.1 us
    ppermute x8, waiting for transfers between devices, shifted(): return lax.ppermute(block, axis, route)  11.2 us
    ppermute x8, starting transfers between devices, shifted(): return lax.ppermute(block, axis, route)  11 us
  transfers between devices with their start and end apart: 10, of which 5 were waited for; matrix products, arithmetic and copies ran while one was open for 11% of the time, Pallas kernels for 0%

commit v1 on v0

--- a/solution.py
+++ b/solution.py
@@ -5,6 +5,18 @@
 
 GY = 4
 STEPS = 2
+
+
+def ring_gather(shard, axis, dim):
+    ways, here, hop = (lax.axis_size(axis), lax.axis_index(axis), shard.shape[dim])
+    shape = [n * ways if d == dim else n for d, n in enumerate(shard.shape)]
+    full = lax.dynamic_update_slice_in_dim(
+        jnp.zeros(shape, shard.dtype), shard, here * hop, axis=dim
+    )
+    for far in range(1, ways):
+        shard = lax.ppermute(shard, axis, [(d, (d + 1) % ways) for d in range(ways)])
+        full = lax.dynamic_update_slice_in_dim(full, shard, (here - far) % ways * hop, axis=dim)
+    return full
 
 
 def shifted(block, axis, distance):
@@ -25,7 +37,7 @@
 
 def scatter_term(rounded, coupling):
     contract = (((1,), (1,)), ((), ()))
-    gathered = lax.all_gather(rounded, "modes", axis=1, tiled=True)
+    gathered = ring_gather(rounded, "modes", 1)
     return lax.dot_general(gathered, coupling, contract, preferred_element_type=jnp.float32)
 
 

time: 520 us -> 492 us (0.946)
  waiting for transfers between devices: 369 us -> 326 us
  local copies, waits for them, and re-layouts: 19.2 us -> 52.8 us
  between operations: 13.8 us -> 0.37 us
  other arithmetic: 58.1 us -> 48.7 us
    all_gather x2 -> x0, waiting for transfers between devices: 358 us -> none  [scatter_term(): gathered = lax.all_gather(rounded, 'modes', axis=1, tiled=True)]
    ppermute x0 -> x6, waiting for transfers between devices: none -> 323 us  [ring_gather(): lax.ppermute(shard, axis, [(d, (d + 1) % ways) for d in range(ways)])]
    dynamic_update_slice x0 -> x8, local copies, waits for them, and re-layouts: none -> 27.1 us  [the longest x6 21 us: ring_gather(): lax.dynamic_update_slice_in_dim(full, shard, (here - far) % ways * hop, a...]
    another operation x0 -> x2, local copies, waits for them, and re-layouts: none -> 12.2 us
    ppermute x8, waiting for transfers between devices: 11.2 us -> 3.39 us  [shifted(): return lax.ppermute(block, axis, route)]
  transfers between devices with their start and end apart: 10 -> 14, of which waited for: 5 -> 7; matrix products, arithmetic and copies ran while one was open for 11% -> 16% of each run, Pallas kernels for 0% -> 0%
where the time goes in v1:
time: 492 us; the launch traced here: 491 us
  waiting for transfers between devices  326 us (66%)
  local copies, waits for them, and re-layouts  52.8 us (11%)
  matrix products  50.6 us (10%)
  other arithmetic  48.7 us (10%)
  starting transfers between devices  11.8 us (2%)
    ppermute x6, waiting for transfers between devices, ring_gather(): lax.ppermute(shard, axis, [(d, (d + 1) % ways) for d in range(ways)])  323 us
    dot_general x2, matrix products, scatter_term(): lax.dot_general(gathered, coupling, contract, preferred_element_type=jnp....  50.6 us
    add x2, other arithmetic, advect(): transport = transport + courant[2] * (density - upstream_z)  25.5 us
    dynamic_update_slice x6, local copies, waits for them, and re-layouts, ring_gather(): lax.dynamic_update_slice_in_dim(full, shard, (here - far) % ways * hop, a...  21 us
    another operation x2, local copies, waits for them, and re-layouts  12.2 us
  transfers between devices with their start and end apart: 14, of which 7 were waited for; matrix products, arithmetic and copies ran while one was open for 16% of the time, Pallas kernels for 0%

profile of v1, /device:TPU:0, one launch (start us, length us, event | category | flops | bytes accessed | tf_op | source)
XLA Modules:
  0.0 490.7 jit_solution(14498961508575347192)
XLA Ops:
  0.0 3.4 convert.12
  3.4 3.1 collective-permute-start.4
  6.5 70.2 %collective-permute-done.4 = bf16[1024,1536]{1,0:T(8,128)(2,1)} collective-permute-done((bf16[1024,1536]{1,0:T(8,128)(2,1)S(1)}, bf16[1024,1536]{1,0:T(8,128)(2,1)}, u32[]{:S(2)}, u32[]{:S(2)}) %collective-permute-start.4) | collective-permute-done | bytes 3145760 | tf_op jit(solution)/shard_map/ppermute | solution.py:17
  86.5 18.3 %fusion.4 = f32[8,8,16,1536]{3,2,1,0:T(8,128)} fusion(f32[8,8,16,1536]{3,2,1,0:T(8,128)} %bitcast.80, f32[1536]{0:T(1024)S(1)} %get-tuple-element.105, f32[1536]{0:T(1024)S(1)} %get-tuple-element.106, f32[1536]{0:T(1024)S(1)} %get-tuple-element.104, pred[1536]{0:T(1024)(128)(4,1)S(1)} %get-tuple-element.102, pred[1536]{0:T(1024)(128)(4,1)S(1)} %get-tuple-element.103, ...), kind=kLoop, calls=%fused_computation.18 | loop fusion | flops 17301504 | bytes 12605952 | tf_op jit(solution)/shard_map/add | solution.py:60
  104.8 43.3 %collective-permute-done.5 = bf16[1024,1536]{1,0:T(8,128)(2,1)} collective-permute-done((bf16[1024,1536]{1,0:T(8,128)(2,1)}, bf16[1024,1536]{1,0:T(8,128)(2,1)}, u32[]{:S(2)}, u32[]{:S(2)}) %collective-permute-start.5) | collective-permute-done | bytes 3145760 | tf_op jit(solution)/shard_map/ppermute | solution.py:17
  148.1 6.1 %broadcast.148.clone = bf16[1024,6144]{1,0:T(8,128)(2,1)} broadcast(bf16[]{:T(256)} %constant.249.clone.1), dimensions={} | broadcast | bytes 12582914 | tf_op jit(solution)/shard_map/broadcast.3
  160.0 3.2 copy.16
  166.3 3.8 constant_dynamic-update-slice_fusion.6
  170.1 3.8 constant_dynamic-update-slice_fusion.5
  173.9 44.7 %collective-permute-done.6 = bf16[1024,1536]{1,0:T(8,128)(2,1)} collective-permute-done((bf16[1024,1536]{1,0:T(8,128)(2,1)}, bf16[1024,1536]{1,0:T(8,128)(2,1)}, u32[]{:S(2)}, u32[]{:S(2)}) %collective-permute-start.6) | collective-permute-done | bytes 3145760 | tf_op jit(solution)/shard_map/ppermute | solution.py:17
  218.6 3.9 constant_dynamic-update-slice_fusion.4
  222.6 26.5 %fusion.37 = f32[1024,1536]{1,0:T(8,128)} fusion(bf16[1024,6144]{1,0:T(8,128)(2,1)} %constant_dynamic-update-slice_fusion.4, bf16[1536,6144]{1,0:T(8,128)(2,1)} %param.29), kind=kOutput, calls=%fused_computation.85 | convolution fusion | flops 19327352832 | bytes 37748736 | tf_op jit(solution)/shard_map/dot_general | solution.py:41
  249.2 4.6 fusion.36
  253.9 69.2 %collective-permute-done.11 = bf16[1024,1536]{1,0:T(8,128)(2,1)S(1)} collective-permute-done((bf16[1024,1536]{1,0:T(8,128)(2,1)S(1)}, bf16[1024,1536]{1,0:T(8,128)(2,1)S(1)}, u32[]{:S(2)}, u32[]{:S(2)}) %collective-permute-start.11) | collective-permute-done | bytes 3145760 | tf_op jit(solution)/shard_map/ppermute | solution.py:17
  325.8 7.2 %fusion.12 = f32[8,8,16,1536]{3,2,1,0:T(8,128)} fusion(f32[8,8,16,1536]{3,2,1,0:T(8,128)S(1)} %get-tuple-element.108, f32[1536]{0:T(1024)S(1)} %copy-done.18, f32[1536]{0:T(1024)S(1)} %copy-done.10, f32[1536]{0:T(1024)S(1)} %copy-done.8, pred[1536]{0:T(1024)(128)(4,1)S(1)} %copy-done.22, pred[1536]{0:T(1024)(128)(4,1)S(1)} %copy-done.12, ...), kind=kLoop, calls=%fused_computation.26 | loop fusion | flops 17301504 | bytes 12605952 | tf_op jit(solution)/shard_map/add | solution.py:60
  333.0 58.5 %collective-permute-done.12 = bf16[1024,1536]{1,0:T(8,128)(2,1)} collective-permute-done((bf16[1024,1536]{1,0:T(8,128)(2,1)S(1)}, bf16[1024,1536]{1,0:T(8,128)(2,1)}, u32[]{:S(2)}, u32[]{:S(2)}) %collective-permute-start.12) | collective-permute-done | bytes 3145760 | tf_op jit(solution)/shard_map/ppermute | solution.py:17
  395.6 6.1 %broadcast.148 = bf16[1024,6144]{1,0:T(8,128)(2,1)} broadcast(bf16[]{:T(256)} %constant.249.clone.1), dimensions={} | broadcast | bytes 12582914 | tf_op jit(solution)/shard_map/broadcast.3
  401.7 4.1 constant_dynamic-update-slice_fusion.3
  408.6 3.4 collective-permute-done.8
  418.3 3.8 constant_dynamic-update-slice_fusion.1
  422.1 37.1 %collective-permute-done.13 = bf16[1024,1536]{1,0:T(8,128)(2,1)} collective-permute-done((bf16[1024,1536]{1,0:T(8,128)(2,1)}, bf16[1024,1536]{1,0:T(8,128)(2,1)}, u32[]{:S(2)}, u32[]{:S(2)}) %collective-permute-start.13) | collective-permute-done | bytes 3145760 | tf_op jit(solution)/shard_map/ppermute | solution.py:17
  459.2 3.8 constant_dynamic-update-slice_fusion
  463.0 24.1 %fusion.38 = f32[1024,1536]{1,0:T(8,128)S(1)} fusion(bf16[1024,6144]{1,0:T(8,128)(2,1)} %constant_dynamic-update-slice_fusion, bf16[1536,6144]{1,0:T(8,128)(2,1)} %param.29), kind=kOutput, calls=%fused_computation.86 | convolution fusion | flops 19327352832 | bytes 37748736 | tf_op jit(solution)/shard_map/dot_general | solution.py:41
  487.1 3.6 fusion.16
  (95 shorter events, 34.5 us)
Async XLA Ops:
  0.0 79.0 %copy-start = (f32[1,8,8,16,1536]{4,3,2,1,0:T(8,128)S(1)}, f32[1,8,8,16,1536]{4,3,2,1,0:T(8,128)}, u32[]{:S(2)}) copy-start(f32[1,8,8,16,1536]{4,3,2,1,0:T(8,128)} %param.23) | copy-start | bytes 18874372
  3.4 73.3 %collective-permute-start.4 = (bf16[1024,1536]{1,0:T(8,128)(2,1)S(1)}, bf16[1024,1536]{1,0:T(8,128)(2,1)}, u32[]{:S(2)}, u32[]{:S(2)}) collective-permute-start(bf16[1024,1536]{1,0:T(8,128)(2,1)S(1)} %bitcast.85), channel_id=1, source_target_pairs={{0,1},{1,2},{2,3},{3,0},{4,5},{5,6},{6,7},{7,4},{8,9},{9,10},{10,1... | collective-permute-start | bytes 9437192 | tf_op jit(solution)/shard_map/ppermute | solution.py:17
  76.7 71.4 %collective-permute-start.5 = (bf16[1024,1536]{1,0:T(8,128)(2,1)}, bf16[1024,1536]{1,0:T(8,128)(2,1)}, u32[]{:S(2)}, u32[]{:S(2)}) collective-permute-start(bf16[1024,1536]{1,0:T(8,128)(2,1)} %collective-permute-done.4), channel_id=1, source_target_pairs={{0,1},{1,2},{2,3},{3,0},{4,5},{5,6},{6,7},{7,4},{8,9},{9,10},{10,1... | collective-permute-start | bytes 9437192 | tf_op jit(solution)/shard_map/ppermute | solution.py:17
  77.5 80.2 %collective-permute-start = (bf16[8,16,1536]{2,1,0:T(8,128)(2,1)}, bf16[8,16,1536]{2,1,0:T(8,128)(2,1)}, u32[]{:S(2)}, u32[]{:S(2)}) collective-permute-start(bf16[8,16,1536]{2,1,0:T(8,128)(2,1)} %slice_bitcast_fusion.10), channel_id=1, source_target_pairs={{16,0},{20,4},{24,8},{28,12},{0,16},{4,20},{8,24},{12,28},{17,1},{... | collective-permute-start | bytes 1179656 | tf_op jit(solution)/shard_map/ppermute | solution.py:25
  80.0 83.3 %collective-permute-start.1 = (f32[8,16,1536]{2,1,0:T(8,128)}, f32[8,16,1536]{2,1,0:T(8,128)}, u32[]{:S(2)}, u32[]{:S(2)}) collective-permute-start(f32[8,16,1536]{2,1,0:T(8,128)} %slice_bitcast_fusion.4), channel_id=1, source_target_pairs={{16,0},{20,4},{24,8},{28,12},{0,16},{4,20},{8,24},{12,28},{17,1},{... | collective-permute-start | bytes 2359304 | tf_op jit(solution)/shard_map/ppermute | solution.py:25
  82.0 82.8 %collective-permute-start.2 = (bf16[8,16,1536]{2,1,0:T(8,128)(2,1)}, bf16[8,16,1536]{2,1,0:T(8,128)(2,1)}, u32[]{:S(2)}, u32[]{:S(2)}) collective-permute-start(bf16[8,16,1536]{2,1,0:T(8,128)(2,1)} %get-tuple-element.112), channel_id=1, source_target_pairs={{28,0},{0,4},{4,8},{8,12},{12,16},{16,20},{20,24},{24,28},{29,1},{... | collective-permute-start | bytes 1179656 | tf_op jit(solution)/shard_map/ppermute | solution.py:25
  82.0 84.1 %collective-permute-start.3 = (bf16[8,16,1536]{2,1,0:T(8,128)(2,1)}, bf16[8,16,1536]{2,1,0:T(8,128)(2,1)S(1)}, u32[]{:S(2)}, u32[]{:S(2)}) collective-permute-start(bf16[8,16,1536]{2,1,0:T(8,128)(2,1)} %get-tuple-element.111), channel_id=1, source_target_pairs={{4,0},{8,4},{12,8},{16,12},{20,16},{24,20},{28,24},{0,28},{5,1},{9... | collective-permute-start | bytes 1179656 | tf_op jit(solution)/shard_map/ppermute | solution.py:25
  85.5 70.7 %copy-start.7 = (f32[1536]{0:T(1024)}, f32[1536]{0:T(1024)S(1)}, u32[]{:S(2)}) copy-start(f32[1536]{0:T(1024)S(1)} %get-tuple-element.104) | copy-start | bytes 18436
  148.1 70.5 %collective-permute-start.6 = (bf16[1024,1536]{1,0:T(8,128)(2,1)}, bf16[1024,1536]{1,0:T(8,128)(2,1)}, u32[]{:S(2)}, u32[]{:S(2)}) collective-permute-start(bf16[1024,1536]{1,0:T(8,128)(2,1)} %collective-permute-done.5), channel_id=1, source_target_pairs={{0,1},{1,2},{2,3},{3,0},{4,5},{5,6},{6,7},{7,4},{8,9},{9,10},{10,1... | collective-permute-start | bytes 9437192 | tf_op jit(solution)/shard_map/ppermute | solution.py:17
  157.7 91.4 %copy-start.5 = (f32[8,8,16]{2,1,0:T(8,128)}, f32[8,8,16]{2,1,0:T(8,128)S(1)}, u32[]{:S(2)}) copy-start(f32[8,8,16]{2,1,0:T(8,128)S(1)} %convert_bitcast_fusion) | copy-start | bytes 12292
  218.6 30.5 %slice-start = ((s8[6291456]{0:T(1024)(128)(4,1)}), s8[4194304]{0:T(1024)(128)(4,1)S(1)}, s32[]{:S(2)}) async-start(s8[6291456]{0:T(1024)(128)(4,1)} %bitcast.81), calls=%async_computation | async-start | bytes 8388608
  222.6 26.6 %copy-start.20 = (f32[1536]{0:T(1024)S(1)}, f32[1536]{0:T(1024)}, u32[]{:S(2)}) copy-start(f32[1536]{0:T(1024)} %param.27) | copy-start | bytes 18436
  249.1 76.6 %copy-start.8 = (f32[1536]{0:T(1024)S(1)}, f32[1536]{0:T(1024)}, u32[]{:S(2)}) copy-start(f32[1536]{0:T(1024)} %copy-done.7) | copy-start | bytes 18436
  249.2 76.6 %copy-start.10 = (f32[1536]{0:T(1024)S(1)}, f32[1536]{0:T(1024)}, u32[]{:S(2)}) copy-start(f32[1536]{0:T(1024)} %copy-done.9) | copy-start | bytes 18436
  249.2 76.6 %copy-start.18 = (f32[1536]{0:T(1024)S(1)}, f32[1536]{0:T(1024)}, u32[]{:S(2)}) copy-start(f32[1536]{0:T(1024)} %copy-done.17) | copy-start | bytes 18436
  249.2 76.6 %copy-start.22 = (pred[1536]{0:T(1024)(128)(4,1)S(1)}, pred[1536]{0:T(1024)(128)(4,1)}, u32[]{:S(2)}) copy-start(pred[1536]{0:T(1024)(128)(4,1)} %copy-done.21) | copy-start | bytes 4612
  253.8 137.7 %copy-start.2 = (bf16[8,8,16,1536]{3,2,1,0:T(8,128)(2,1)}, bf16[8,8,16,1536]{3,2,1,0:T(8,128)(2,1)S(1)}, u32[]{:S(2)}) copy-start(bf16[8,8,16,1536]{3,2,1,0:T(8,128)(2,1)S(1)} %get-tuple-element.107) | copy-start | bytes 9437188
  253.8 69.3 %collective-permute-start.11 = (bf16[1024,1536]{1,0:T(8,128)(2,1)S(1)}, bf16[1024,1536]{1,0:T(8,128)(2,1)S(1)}, u32[]{:S(2)}, u32[]{:S(2)}) collective-permute-start(bf16[1024,1536]{1,0:T(8,128)(2,1)S(1)} %bitcast.83), channel_id=1, source_target_pairs={{0,1},{1,2},{2,3},{3,0},{4,5},{5,6},{6,7},{7,4},{8,9},{9,10},{10,1... | collective-permute-start | bytes 9437192 | tf_op jit(solution)/shard_map/ppermute | solution.py:17
  323.1 68.4 %collective-permute-start.12 = (bf16[1024,1536]{1,0:T(8,128)(2,1)S(1)}, bf16[1024,1536]{1,0:T(8,128)(2,1)}, u32[]{:S(2)}, u32[]{:S(2)}) collective-permute-start(bf16[1024,1536]{1,0:T(8,128)(2,1)S(1)} %collective-permute-done.11), channel_id=1, source_target_pairs={{0,1},{1,2},{2,3},{3,0},{4,5},{5,6},{6,7},{7,4},{8,9},{9,10},{10,1... | collective-permute-start | bytes 9437192 | tf_op jit(solution)/shard_map/ppermute | solution.py:17
  323.9 81.8 %collective-permute-start.7 = (bf16[8,16,1536]{2,1,0:T(8,128)(2,1)}, bf16[8,16,1536]{2,1,0:T(8,128)(2,1)}, u32[]{:S(2)}, u32[]{:S(2)}) collective-permute-start(bf16[8,16,1536]{2,1,0:T(8,128)(2,1)} %slice_bitcast_fusion.7), channel_id=1, source_target_pairs={{16,0},{20,4},{24,8},{28,12},{0,16},{4,20},{8,24},{12,28},{17,1},{... | collective-permute-start | bytes 1179656 | tf_op jit(solution)/shard_map/ppermute | solution.py:25
  391.5 67.7 %collective-permute-start.13 = (bf16[1024,1536]{1,0:T(8,128)(2,1)}, bf16[1024,1536]{1,0:T(8,128)(2,1)}, u32[]{:S(2)}, u32[]{:S(2)}) collective-permute-start(bf16[1024,1536]{1,0:T(8,128)(2,1)} %collective-permute-done.12), channel_id=1, source_target_pairs={{0,1},{1,2},{2,3},{3,0},{4,5},{5,6},{6,7},{7,4},{8,9},{9,10},{10,1... | collective-permute-start | bytes 9437192 | tf_op jit(solution)/shard_map/ppermute | solution.py:17
  392.4 19.6 %collective-permute-start.8 = (f32[8,16,1536]{2,1,0:T(8,128)}, f32[8,16,1536]{2,1,0:T(8,128)}, u32[]{:S(2)}, u32[]{:S(2)}) collective-permute-start(f32[8,16,1536]{2,1,0:T(8,128)} %slice_bitcast_fusion.1), channel_id=1, source_target_pairs={{16,0},{20,4},{24,8},{28,12},{0,16},{4,20},{8,24},{12,28},{17,1},{... | collective-permute-start | bytes 2359304 | tf_op jit(solution)/shard_map/ppermute | solution.py:25
  393.0 20.3 %collective-permute-start.9 = (bf16[8,16,1536]{2,1,0:T(8,128)(2,1)}, bf16[8,16,1536]{2,1,0:T(8,128)(2,1)}, u32[]{:S(2)}, u32[]{:S(2)}) collective-permute-start(bf16[8,16,1536]{2,1,0:T(8,128)(2,1)} %get-tuple-element.110), channel_id=1, source_target_pairs={{28,0},{0,4},{4,8},{8,12},{12,16},{16,20},{20,24},{24,28},{29,1},{... | collective-permute-start | bytes 1179656 | tf_op jit(solution)/shard_map/ppermute | solution.py:25
  393.0 22.1 %collective-permute-start.10 = (bf16[8,16,1536]{2,1,0:T(8,128)(2,1)}, bf16[8,16,1536]{2,1,0:T(8,128)(2,1)S(1)}, u32[]{:S(2)}, u32[]{:S(2)}) collective-permute-start(bf16[8,16,1536]{2,1,0:T(8,128)(2,1)} %get-tuple-element.109), channel_id=1, source_target_pairs={{4,0},{8,4},{12,8},{16,12},{20,16},{24,20},{28,24},{0,28},{5,1},{9... | collective-permute-start | bytes 1179656 | tf_op jit(solution)/shard_map/ppermute | solution.py:25
  (15 other events, 211.1 us)
